TPU v7x, 32 devices: a whole 2x2x4 slice. The times are simulated.
32 devices in a mesh: gx: 2 (over x), gy: 4 (over z), gz: 4 (over y, core).
Axes of the slice: x: 2, y: 2, z: 4, core: 2. Of those that a mesh axis runs over, the one named last changes fastest.
Arguments:
- source_field: float32 [3, 16, 32, 512], P(None, 'gx', 'gy', 'gz'), may hold values from -6 to 6
- cell_contrast: bfloat16 [4096, 1536], P(('gx', 'gy', 'gz')), may hold values from 0.19921875 to 2
- point_field: bfloat16 [3, 4096], P(None, ('gx', 'gy', 'gz')), may hold values from -3 to 3
- point_class: int32 [4096, 1], P(('gx', 'gy', 'gz')), may hold values from 0 to 1; in each aligned block of 128 rows (0 to 127, 128 to 255, ...) at most 128 rows name the same one
- cell_kind: int32 [4096], P(('gx', 'gy', 'gz')), may hold values from 0 to 3
- inverse_blocks: float32 [2, 4, 3, 3, 512], P('gx'), may hold values from -0.3 to 0.3
Outputs:
- newton_step: float32 [3, 16, 32, 512], P(None, 'gx', 'gy', 'gz')
- krylov_residual: float32 [3, 16, 32, 512], P(None, 'gx', 'gy', 'gz')
Inputs may be any that keep to these rules, and one draw needn't show every extreme that they name: `point_class`: among the 128 points of one device's block no class is named more than 128 times, a bound that some block reaches there.
All inputs are finite; a program needn't handle non-finite values.
Results may differ from a plain program's by a relative error of at most 0.0076.
Values may be sent and summed in bfloat16 or wider, within the bound.
No kernel may reach another device: no remote copies, remote signals or barrier semaphores. Data moves between devices by JAX's collectives and lax.ppermute only.
A program may use at most 64 MiB of HBM per device.

v0:
```python
import math
import jax
import jax.numpy as jnp
from jax import lax
from jax.sharding import PartitionSpec as P

CELL = 8
VOX = 512
TYPES = 4
ZP = 8
ITERS = 3
kerr_scale = 0.1


def with_halo(block, sides, width):
    for axis, dim in sides:
        count = lax.axis_size(axis)
        forward = [(i, i + 1) for i in range(count - 1)]
        backward = [(target, source) for source, target in forward]
        low = lax.ppermute(
            lax.slice_in_dim(block, block.shape[dim] - width, None, axis=dim), axis, forward
        )
        high = lax.ppermute(lax.slice_in_dim(block, 0, width, axis=dim), axis, backward)
        block = jnp.concatenate([low, block, high], axis=dim)
    return block


def hartley_table():
    voxel_index = jnp.arange(VOX, dtype=jnp.int32)
    along_one = voxel_index // (CELL * CELL)
    along_two = voxel_index // CELL % CELL
    along_three = voxel_index % CELL
    phase_index = (
        along_one[:, None] * along_one[None, :]
        + along_two[:, None] * along_two[None, :]
        + along_three[:, None] * along_three[None, :]
    ) % CELL
    phase_angle = 2.0 * math.pi / CELL * phase_index.astype(jnp.float32)
    return ((jnp.cos(phase_angle) + jnp.sin(phase_angle)) / math.sqrt(VOX)).astype(jnp.bfloat16)


def cell_solve(contrast, point_values, blocks, hartley):
    row_count = contrast.shape[0]
    weights = contrast.reshape(row_count, 3, VOX).astype(jnp.float32)
    base_field = point_values.astype(jnp.float32)[:, :, None]

    def correction(polarization):
        spectrum = jnp.dot(
            polarization.reshape(row_count * 3, VOX), hartley, preferred_element_type=jnp.float32
        ).reshape(row_count, 3, VOX)
        mixed_spectrum = jnp.sum(blocks * spectrum[:, None, :, :], axis=2).astype(jnp.bfloat16)
        return jnp.dot(
            mixed_spectrum.reshape(row_count * 3, VOX), hartley, preferred_element_type=jnp.float32
        ).reshape(row_count, 3, VOX)

    local_field = base_field - correction((weights * base_field).astype(jnp.bfloat16))
    kerr_polar = (weights * local_field * (1.0 + kerr_scale * local_field * local_field)).astype(
        jnp.bfloat16
    )
    final_field = base_field - correction(kerr_polar)
    flux_mean = jnp.mean((1.0 + weights) * final_field, axis=2)
    stiffness = 0.5 + jnp.mean(weights * final_field * final_field, axis=(1, 2))
    return jnp.concatenate([flux_mean, stiffness[:, None]], axis=1)


def solve_batched(contrast, point_values, keys, library, hartley):
    return cell_solve(contrast, point_values, library[keys], hartley)


def operate(field, diagonal):
    padded = with_halo(field, (("gx", 1), ("gy", 2), ("gz", 3)), 1)
    beside = padded[:, 2:, 1:-1, 1:-1] + padded[:, :-2, 1:-1, 1:-1]
    beside = beside + padded[:, 1:-1, 2:, 1:-1] + padded[:, 1:-1, :-2, 1:-1]
    beside = beside + padded[:, 1:-1, 1:-1, 2:] + padded[:, 1:-1, 1:-1, :-2]
    return (6.0 + diagonal)[None] * field - beside


def two_products(residual, image):
    return lax.psum((jnp.sum(residual * residual), jnp.sum(residual * image)), ("gx", "gy", "gz"))


def per_device(source_field, cell_contrast, point_field, point_class, cell_kind, inverse_blocks):
    hartley = hartley_table()
    point_values = point_field.T
    library = lax.all_gather(inverse_blocks, "gx", axis=0, tiled=True)
    library = library.reshape(library.shape[0] * library.shape[1], 3, 3, VOX)
    chosen = point_class[:, 0] * TYPES + cell_kind
    summary = solve_batched(cell_contrast, point_values, chosen, library, hartley)
    extent_x = source_field.shape[1]
    extent_y = source_field.shape[2]
    extent_z = source_field.shape[3]
    blocks_z = extent_z // ZP
    stiffness_grid = jnp.broadcast_to(
        summary[:, 3].reshape(1, extent_y, blocks_z, 1), (extent_x, extent_y, blocks_z, ZP)
    ).reshape(extent_x, extent_y, extent_z)
    flux_grid = jnp.broadcast_to(
        summary[:, :3].T.reshape(3, 1, extent_y, blocks_z, 1), (3, extent_x, extent_y, blocks_z, ZP)
    ).reshape(3, extent_x, extent_y, extent_z)
    right = source_field - flux_grid
    newton_step = jnp.zeros_like(right)
    residual = right
    image = operate(residual, stiffness_grid)
    norm_now, product = two_products(residual, image)
    alpha = norm_now / product
    direction, along = (residual, image)
    for iteration in range(ITERS):
        newton_step = newton_step + alpha * direction
        residual = residual - alpha * along
        if iteration + 1 < ITERS:
            image = operate(residual, stiffness_grid)
            norm_next, product = two_products(residual, image)
            ratio = norm_next / norm_now
            alpha = norm_next / (product - ratio * norm_next / alpha)
            direction = residual + ratio * direction
            along = image + ratio * along
            norm_now = norm_next
    return (newton_step, residual)


def solution(mesh):
    placed = (
        P(None, "gx", "gy", "gz"),
        P(("gx", "gy", "gz"), None),
        P(None, ("gx", "gy", "gz")),
        P(("gx", "gy", "gz"), None),
        P(("gx", "gy", "gz")),
        P("gx", None, None, None, None),
    )
    return jax.shard_map(
        per_device,
        mesh=mesh,
        in_specs=placed,
        out_specs=(P(None, "gx", "gy", "gz"), P(None, "gx", "gy", "gz")),
        check_vma=False,
    )
```

profile of v0, /device:TPU:0, one launch (start us, length us, event | category | flops | bytes accessed | tf_op | source)
XLA Modules:
  0.0 260.3 jit_solution(5146362177927208598)
XLA Ops:
  0.7 0.7 convert_bitcast_fusion
  1.3 0.7 compare_select_fusion
  2.0 6.2 %all_gather.3 = f32[2,4,3,3,512]{4,1,3,2,0:T(4,128)S(1)} all-gather(f32[1,4,3,3,512]{4,1,3,2,0:T(4,128)} %param.11), channel_id=1, replica_groups=mesh['gx'=2,'gy'=4,'gz'=4] {'gx'}, dimensions={0}, use_global_device_ids=true | all-gather | bytes 221184 | tf_op jit(solution)/shard_map/all_gather | solution.py:85
  8.2 0.1 copy.45
  8.3 1.2 copy.34
  9.6 0.2 copy.35
  9.8 4.7 %fusion.12 = f32[128,3,512]{2,0,1:T(8,128)S(1)} fusion(s32[512]{0:T(512)S(1)} %get-tuple-element.39, s32[512]{0:T(512)S(1)} %get-tuple-element.40, s32[512]{0:T(512)S(1)} %add_select_fusion.4, f32[128,3,512]{2,0,1:T(8,128)S(1)} %copy.35, f32[128,3]{0,1:T(4,128)S(1)} %convert_bitcast_fusion), kind=kOutput, calls=%fused_computation.24 | convolution fusion | flops 207224832 | bytes 1580544 | tf_op jit(solution)/shard_map/dot_general | solution.py:48
  14.5 1.5 copy.39
  16.0 2.4 gather_fusion
  18.5 4.6 %multiply_reduce_fusion.1 = bf16[128,3,512]{2,1,0:T(4,128)(2,1)} fusion(f32[128,3,3,512]{3,2,1,0:T(4,128)S(1)} %gather_fusion, f32[128,3,512]{2,1,0:T(4,128)} %copy.39), kind=kLoop, calls=%fused_computation.2 | loop fusion | flops 983040 | bytes 3538944 | tf_op jit(solution)/shard_map/reduce_sum | solution.py:51
  23.1 11.6 %fusion.7 = f32[128,3,512]{2,0,1:T(8,128)} fusion(f32[128,3,512]{2,0,1:T(8,128)} %copy-done.1, s32[512]{0:T(512)S(1)} %get-tuple-element.39, s32[512]{0:T(512)S(1)} %get-tuple-element.40, s32[512]{0:T(512)S(1)} %add_select_fusion.4, bf16[128,3,512]{2,1,0:T(4,128)(2,1)} %multiply_reduce_fusion.1, f32[128,3]{0,1:T(4,128)S(1)} %convert_bitcast_fusion), kind=kOutput, calls=%fused_computation.21 | convolution fusion | flops 415039488 | bytes 1973760 | tf_op jit(solution)/shard_map/dot_general | solution.py:48
  34.7 1.7 copy.42
  36.5 3.5 %multiply_reduce_fusion = bf16[128,3,512]{2,1,0:T(4,128)(2,1)S(1)} fusion(f32[128,3,3,512]{3,2,1,0:T(4,128)S(1)} %gather_fusion, f32[128,3,512]{2,1,0:T(4,128)S(1)} %copy.42), kind=kLoop, calls=%fused_computation.1 | loop fusion | flops 983040 | bytes 3538944 | tf_op jit(solution)/shard_map/reduce_sum | solution.py:51
  39.9 5.2 %fusion.6 = (f32[128]{0:T(128)S(1)}, f32[128,3]{0,1:T(4,128)S(1)}) fusion(f32[128,3,512]{2,0,1:T(8,128)S(1)} %copy-done.2, s32[512]{0:T(512)S(1)} %get-tuple-element.39, s32[512]{0:T(512)S(1)} %get-tuple-element.40, s32[512]{0:T(512)S(1)} %add_select_fusion.4, bf16[128,3,512]{2,1,0:T(4,128)(2,1)S(1)} %multiply_reduce_fusion, ...), kind=kOutput, calls=%fused_computation.17 | convolution fusion | flops 208207360 | bytes 1189376 | tf_op jit(solution)/shard_map/dot_general | solution.py:52
  45.1 0.1 broadcast_in_dim.13
  45.2 0.1 broadcast_in_dim.14
  45.3 0.1 broadcast_in_dim.15
  45.5 3.9 %collective-permute-start.1 = (f32[3,1,8,128]{3,2,1,0:T(8,128)S(1)}, f32[3,1,8,128]{3,2,1,0:T(8,128)S(1)}, u32[]{:S(2)}, u32[]{:S(2)}) collective-permute-start(f32[3,1,8,128]{3,2,1,0:T(8,128)S(1)} %get-tuple-element.37), channel_id=1, source_target_pairs={{0,16},{1,17},{2,18},{3,19},{4,20},{5,21},{6,22},{7,23},{8,24},{9,... | collective-permute-start | bytes 36872 | tf_op jit(solution)/shard_map/ppermute | solution.py:20
  49.4 1.3 collective-permute-start
  50.7 0.1 collective-permute-done.1
  50.8 4.2 %collective-permute-done = f32[3,1,8,128]{3,2,1,0:T(8,128)S(1)} collective-permute-done((f32[3,1,8,128]{3,2,1,0:T(8,128)S(1)}, f32[3,1,8,128]{3,2,1,0:T(8,128)S(1)}, u32[]{:S(2)}, u32[]{:S(2)}) %collective-permute-start) | collective-permute-done | bytes 12320 | tf_op jit(solution)/shard_map/ppermute | solution.py:23
  55.0 3.5 %collective-permute-start.3 = (f32[3,10,1,128]{3,2,1,0:T(1,128)S(1)}, f32[3,10,1,128]{3,2,1,0:T(1,128)S(1)}, u32[]{:S(2)}, u32[]{:S(2)}) collective-permute-start(f32[3,10,1,128]{3,2,1,0:T(1,128)S(1)} %get-tuple-element.29), channel_id=1, source_target_pairs={{0,4},{4,8},{8,12},{1,5},{5,9},{9,13},{2,6},{6,10},{10,14},{3,7},{... | collective-permute-start | bytes 46088 | tf_op jit(solution)/shard_map/ppermute | solution.py:20
  58.5 1.3 collective-permute-start.2
  59.8 0.1 collective-permute-done.3
  59.9 4.2 %collective-permute-done.2 = f32[3,10,1,128]{3,2,1,0:T(1,128)S(1)} collective-permute-done((f32[3,10,1,128]{3,2,1,0:T(1,128)S(1)}, f32[3,10,1,128]{3,2,1,0:T(1,128)S(1)}, u32[]{:S(2)}, u32[]{:S(2)}) %collective-permute-start.2) | collective-permute-done | bytes 15392 | tf_op jit(solution)/shard_map/ppermute | solution.py:23
  64.1 0.1 pad_maximum_fusion
  64.1 0.1 fusion.70
  64.3 1.3 collective-permute-start.4
  65.6 3.0 %collective-permute-start.5 = (f32[3,10,10,1]{3,2,1,0:T(8,128)S(1)}, f32[3,10,10,1]{3,2,1,0:T(8,128)S(1)}, u32[]{:S(2)}, u32[]{:S(2)}) collective-permute-start(f32[3,10,10,1]{3,2,1,0:T(8,128)S(1)} %get-tuple-element.24), channel_id=1, source_target_pairs={{0,1},{1,2},{2,3},{4,5},{5,6},{6,7},{8,9},{9,10},{10,11},{12,13},{... | collective-permute-start | bytes 3608 | tf_op jit(solution)/shard_map/ppermute | solution.py:20
  68.6 0.1 add.222
  68.7 0.1 broadcast_in_dim.34
  68.8 0.1 add.223
  68.9 0.8 collective-permute-done.5
  69.7 0.8 multiply_reduce_fusion.7
  70.5 43.3 %all-reduce.2 = (f32[]{:T(128)}, f32[]{:T(128)}) all-reduce(f32[]{:T(128)} %get-tuple-element.9, f32[]{:T(128)} %get-tuple-element.8), channel_id=1, replica_groups=mesh['gx'=2,'gy'=4,'gz'=4] {'gx','gy','gz'}, use_global_device_ids=true, to_apply=%region_4.5 | all-reduce | flops 2 | bytes 16 | tf_op jit(solution)/shard_map/psum | solution.py:79
  115.2 4.2 %collective-permute-start.7 = (f32[3,1,8,128]{3,2,1,0:T(8,128)S(1)}, f32[3,1,8,128]{3,2,1,0:T(8,128)S(1)}, u32[]{:S(2)}, u32[]{:S(2)}) collective-permute-start(f32[3,1,8,128]{3,2,1,0:T(8,128)S(1)} %get-tuple-element.35), channel_id=1, source_target_pairs={{0,16},{1,17},{2,18},{3,19},{4,20},{5,21},{6,22},{7,23},{8,24},{9,... | collective-permute-start | bytes 36872 | tf_op jit(solution)/shard_map/ppermute | solution.py:20
  119.4 1.3 collective-permute-start.6
  120.7 0.1 collective-permute-done.7
  120.7 4.2 %collective-permute-done.6 = f32[3,1,8,128]{3,2,1,0:T(8,128)S(1)} collective-permute-done((f32[3,1,8,128]{3,2,1,0:T(8,128)S(1)}, f32[3,1,8,128]{3,2,1,0:T(8,128)S(1)}, u32[]{:S(2)}, u32[]{:S(2)}) %collective-permute-start.6) | collective-permute-done | bytes 12320 | tf_op jit(solution)/shard_map/ppermute | solution.py:23
  125.0 2.1 collective-permute-start.9
  127.1 1.3 collective-permute-start.8
  128.4 0.1 collective-permute-done.9
  128.5 4.2 %collective-permute-done.8 = f32[3,10,1,128]{3,2,1,0:T(1,128)S(1)} collective-permute-done((f32[3,10,1,128]{3,2,1,0:T(1,128)S(1)}, f32[3,10,1,128]{3,2,1,0:T(1,128)S(1)}, u32[]{:S(2)}, u32[]{:S(2)}) %collective-permute-start.8) | collective-permute-done | bytes 15392 | tf_op jit(solution)/shard_map/ppermute | solution.py:23
  132.7 0.1 fusion.69
  132.9 1.3 collective-permute-start.10
  134.2 3.0 %collective-permute-start.11 = (f32[3,10,10,1]{3,2,1,0:T(8,128)S(1)}, f32[3,10,10,1]{3,2,1,0:T(8,128)S(1)}, u32[]{:S(2)}, u32[]{:S(2)}) collective-permute-start(f32[3,10,10,1]{3,2,1,0:T(8,128)S(1)} %get-tuple-element.22), channel_id=1, source_target_pairs={{0,1},{1,2},{2,3},{4,5},{5,6},{6,7},{8,9},{9,10},{10,11},{12,13},{... | collective-permute-start | bytes 3608 | tf_op jit(solution)/shard_map/ppermute | solution.py:20
  137.2 1.1 collective-permute-done.11
  138.3 0.8 multiply_reduce_fusion.5
  139.2 43.9 %all-reduce.1 = (f32[]{:T(128)}, f32[]{:T(128)}) all-reduce(f32[]{:T(128)} %get-tuple-element.7, f32[]{:T(128)} %get-tuple-element.6), channel_id=1, replica_groups=mesh['gx'=2,'gy'=4,'gz'=4] {'gx','gy','gz'}, use_global_device_ids=true, to_apply=%region_9.10 | all-reduce | flops 2 | bytes 16 | tf_op jit(solution)/shard_map/psum | solution.py:79
  187.6 4.2 %collective-permute-start.13 = (f32[3,1,8,128]{3,2,1,0:T(8,128)S(1)}, f32[3,1,8,128]{3,2,1,0:T(8,128)S(1)}, u32[]{:S(2)}, u32[]{:S(2)}) collective-permute-start(f32[3,1,8,128]{3,2,1,0:T(8,128)S(1)} %get-tuple-element.33), channel_id=1, source_target_pairs={{0,16},{1,17},{2,18},{3,19},{4,20},{5,21},{6,22},{7,23},{8,24},{9,... | collective-permute-start | bytes 36872 | tf_op jit(solution)/shard_map/ppermute | solution.py:20
  191.8 1.3 collective-permute-start.12
  193.1 0.1 collective-permute-done.13
  193.2 4.2 %collective-permute-done.12 = f32[3,1,8,128]{3,2,1,0:T(8,128)S(1)} collective-permute-done((f32[3,1,8,128]{3,2,1,0:T(8,128)S(1)}, f32[3,1,8,128]{3,2,1,0:T(8,128)S(1)}, u32[]{:S(2)}, u32[]{:S(2)}) %collective-permute-start.12) | collective-permute-done | bytes 12320 | tf_op jit(solution)/shard_map/ppermute | solution.py:23
  197.4 2.1 collective-permute-start.15
  199.5 1.3 collective-permute-start.14
  200.8 0.1 collective-permute-done.15
  200.9 4.2 %collective-permute-done.14 = f32[3,10,1,128]{3,2,1,0:T(1,128)S(1)} collective-permute-done((f32[3,10,1,128]{3,2,1,0:T(1,128)S(1)}, f32[3,10,1,128]{3,2,1,0:T(1,128)S(1)}, u32[]{:S(2)}, u32[]{:S(2)}) %collective-permute-start.14) | collective-permute-done | bytes 15392 | tf_op jit(solution)/shard_map/ppermute | solution.py:23
  205.2 0.1 fusion.68
  205.3 1.3 collective-permute-start.16
  206.6 3.0 %collective-permute-start.17 = (f32[3,10,10,1]{3,2,1,0:T(8,128)S(1)}, f32[3,10,10,1]{3,2,1,0:T(8,128)S(1)}, u32[]{:S(2)}, u32[]{:S(2)}) collective-permute-start(f32[3,10,10,1]{3,2,1,0:T(8,128)S(1)} %get-tuple-element.20), channel_id=1, source_target_pairs={{0,1},{1,2},{2,3},{4,5},{5,6},{6,7},{8,9},{9,10},{10,11},{12,13},{... | collective-permute-start | bytes 3608 | tf_op jit(solution)/shard_map/ppermute | solution.py:20
  209.7 1.1 collective-permute-done.17
  210.8 0.8 multiply_reduce_fusion.3
  211.6 44.0 %all-reduce = (f32[]{:T(128)}, f32[]{:T(128)}) all-reduce(f32[]{:T(128)} %get-tuple-element.5, f32[]{:T(128)} %get-tuple-element.4), channel_id=1, replica_groups=mesh['gx'=2,'gy'=4,'gz'=4] {'gx','gy','gz'}, use_global_device_ids=true, to_apply=%region_13.14 | all-reduce | flops 2 | bytes 16 | tf_op jit(solution)/shard_map/psum | solution.py:79
  259.5 0.7 multiply_subtract_fusion
  (25 shorter events, 0.3 us)
Async XLA Ops:
  9.7 4.8 %copy-start.1 = (f32[128,3,512]{2,0,1:T(8,128)}, f32[128,3,512]{2,0,1:T(8,128)S(1)}, u32[]{:S(2)}) copy-start(f32[128,3,512]{2,0,1:T(8,128)S(1)} %copy.35) | copy-start | bytes 2359300
  34.7 5.2 %copy-start.2 = (f32[128,3,512]{2,0,1:T(8,128)S(1)}, f32[128,3,512]{2,0,1:T(8,128)}, u32[]{:S(2)}) copy-start(f32[128,3,512]{2,0,1:T(8,128)} %copy-done.1) | copy-start | bytes 2359300
  39.9 5.5 %copy-start = (f32[3,8,8,128]{3,2,1,0:T(8,128)S(1)}, f32[3,8,8,128]{3,2,1,0:T(8,128)}, u32[]{:S(2)}) copy-start(f32[3,8,8,128]{3,2,1,0:T(8,128)} %param.6) | copy-start | bytes 294916
  45.5 5.3 %collective-permute-start.1 = (f32[3,1,8,128]{3,2,1,0:T(8,128)S(1)}, f32[3,1,8,128]{3,2,1,0:T(8,128)S(1)}, u32[]{:S(2)}, u32[]{:S(2)}) collective-permute-start(f32[3,1,8,128]{3,2,1,0:T(8,128)S(1)} %get-tuple-element.37), channel_id=1, source_target_pairs={{0,16},{1,17},{2,18},{3,19},{4,20},{5,21},{6,22},{7,23},{8,24},{9,... | collective-permute-start | bytes 36872 | tf_op jit(solution)/shard_map/ppermute | solution.py:20
  49.4 5.6 %collective-permute-start = (f32[3,1,8,128]{3,2,1,0:T(8,128)S(1)}, f32[3,1,8,128]{3,2,1,0:T(8,128)S(1)}, u32[]{:S(2)}, u32[]{:S(2)}) collective-permute-start(f32[3,1,8,128]{3,2,1,0:T(8,128)S(1)} %get-tuple-element.38), channel_id=1, source_target_pairs={{16,0},{17,1},{18,2},{19,3},{20,4},{21,5},{22,6},{23,7},{24,8},{25... | collective-permute-start | bytes 36872 | tf_op jit(solution)/shard_map/ppermute | solution.py:23
  55.0 4.9 %collective-permute-start.3 = (f32[3,10,1,128]{3,2,1,0:T(1,128)S(1)}, f32[3,10,1,128]{3,2,1,0:T(1,128)S(1)}, u32[]{:S(2)}, u32[]{:S(2)}) collective-permute-start(f32[3,10,1,128]{3,2,1,0:T(1,128)S(1)} %get-tuple-element.29), channel_id=1, source_target_pairs={{0,4},{4,8},{8,12},{1,5},{5,9},{9,13},{2,6},{6,10},{10,14},{3,7},{... | collective-permute-start | bytes 46088 | tf_op jit(solution)/shard_map/ppermute | solution.py:20
  58.5 5.6 %collective-permute-start.2 = (f32[3,10,1,128]{3,2,1,0:T(1,128)S(1)}, f32[3,10,1,128]{3,2,1,0:T(1,128)S(1)}, u32[]{:S(2)}, u32[]{:S(2)}) collective-permute-start(f32[3,10,1,128]{3,2,1,0:T(1,128)S(1)} %get-tuple-element.30), channel_id=1, source_target_pairs={{4,0},{8,4},{12,8},{5,1},{9,5},{13,9},{6,2},{10,6},{14,10},{7,3},{... | collective-permute-start | bytes 46088 | tf_op jit(solution)/shard_map/ppermute | solution.py:23
  64.3 4.6 %collective-permute-start.4 = (f32[3,10,10,1]{3,2,1,0:T(8,128)S(1)}, f32[3,10,10,1]{3,2,1,0:T(8,128)S(1)}, u32[]{:S(2)}, u32[]{:S(2)}) collective-permute-start(f32[3,10,10,1]{3,2,1,0:T(8,128)S(1)} %get-tuple-element.23), channel_id=1, source_target_pairs={{1,0},{2,1},{3,2},{5,4},{6,5},{7,6},{9,8},{10,9},{11,10},{13,12},{... | collective-permute-start | bytes 3608 | tf_op jit(solution)/shard_map/ppermute | solution.py:23
  65.6 4.2 %collective-permute-start.5 = (f32[3,10,10,1]{3,2,1,0:T(8,128)S(1)}, f32[3,10,10,1]{3,2,1,0:T(8,128)S(1)}, u32[]{:S(2)}, u32[]{:S(2)}) collective-permute-start(f32[3,10,10,1]{3,2,1,0:T(8,128)S(1)} %get-tuple-element.24), channel_id=1, source_target_pairs={{0,1},{1,2},{2,3},{4,5},{5,6},{6,7},{8,9},{9,10},{10,11},{12,13},{... | collective-permute-start | bytes 3608 | tf_op jit(solution)/shard_map/ppermute | solution.py:20
  115.2 5.6 %collective-permute-start.7 = (f32[3,1,8,128]{3,2,1,0:T(8,128)S(1)}, f32[3,1,8,128]{3,2,1,0:T(8,128)S(1)}, u32[]{:S(2)}, u32[]{:S(2)}) collective-permute-start(f32[3,1,8,128]{3,2,1,0:T(8,128)S(1)} %get-tuple-element.35), channel_id=1, source_target_pairs={{0,16},{1,17},{2,18},{3,19},{4,20},{5,21},{6,22},{7,23},{8,24},{9,... | collective-permute-start | bytes 36872 | tf_op jit(solution)/shard_map/ppermute | solution.py:20
  119.4 5.6 %collective-permute-start.6 = (f32[3,1,8,128]{3,2,1,0:T(8,128)S(1)}, f32[3,1,8,128]{3,2,1,0:T(8,128)S(1)}, u32[]{:S(2)}, u32[]{:S(2)}) collective-permute-start(f32[3,1,8,128]{3,2,1,0:T(8,128)S(1)} %get-tuple-element.36), channel_id=1, source_target_pairs={{16,0},{17,1},{18,2},{19,3},{20,4},{21,5},{22,6},{23,7},{24,8},{25... | collective-permute-start | bytes 36872 | tf_op jit(solution)/shard_map/ppermute | solution.py:23
  125.0 3.5 %collective-permute-start.9 = (f32[3,10,1,128]{3,2,1,0:T(1,128)S(1)}, f32[3,10,1,128]{3,2,1,0:T(1,128)S(1)}, u32[]{:S(2)}, u32[]{:S(2)}) collective-permute-start(f32[3,10,1,128]{3,2,1,0:T(1,128)S(1)} %get-tuple-element.27), channel_id=1, source_target_pairs={{0,4},{4,8},{8,12},{1,5},{5,9},{9,13},{2,6},{6,10},{10,14},{3,7},{... | collective-permute-start | bytes 46088 | tf_op jit(solution)/shard_map/ppermute | solution.py:20
  127.1 5.6 %collective-permute-start.8 = (f32[3,10,1,128]{3,2,1,0:T(1,128)S(1)}, f32[3,10,1,128]{3,2,1,0:T(1,128)S(1)}, u32[]{:S(2)}, u32[]{:S(2)}) collective-permute-start(f32[3,10,1,128]{3,2,1,0:T(1,128)S(1)} %get-tuple-element.28), channel_id=1, source_target_pairs={{4,0},{8,4},{12,8},{5,1},{9,5},{13,9},{6,2},{10,6},{14,10},{7,3},{... | collective-permute-start | bytes 46088 | tf_op jit(solution)/shard_map/ppermute | solution.py:23
  132.9 4.4 %collective-permute-start.10 = (f32[3,10,10,1]{3,2,1,0:T(8,128)S(1)}, f32[3,10,10,1]{3,2,1,0:T(8,128)S(1)}, u32[]{:S(2)}, u32[]{:S(2)}) collective-permute-start(f32[3,10,10,1]{3,2,1,0:T(8,128)S(1)} %get-tuple-element.21), channel_id=1, source_target_pairs={{1,0},{2,1},{3,2},{5,4},{6,5},{7,6},{9,8},{10,9},{11,10},{13,12},{... | collective-permute-start | bytes 3608 | tf_op jit(solution)/shard_map/ppermute | solution.py:23
  134.2 4.2 %collective-permute-start.11 = (f32[3,10,10,1]{3,2,1,0:T(8,128)S(1)}, f32[3,10,10,1]{3,2,1,0:T(8,128)S(1)}, u32[]{:S(2)}, u32[]{:S(2)}) collective-permute-start(f32[3,10,10,1]{3,2,1,0:T(8,128)S(1)} %get-tuple-element.22), channel_id=1, source_target_pairs={{0,1},{1,2},{2,3},{4,5},{5,6},{6,7},{8,9},{9,10},{10,11},{12,13},{... | collective-permute-start | bytes 3608 | tf_op jit(solution)/shard_map/ppermute | solution.py:20
  187.6 5.6 %collective-permute-start.13 = (f32[3,1,8,128]{3,2,1,0:T(8,128)S(1)}, f32[3,1,8,128]{3,2,1,0:T(8,128)S(1)}, u32[]{:S(2)}, u32[]{:S(2)}) collective-permute-start(f32[3,1,8,128]{3,2,1,0:T(8,128)S(1)} %get-tuple-element.33), channel_id=1, source_target_pairs={{0,16},{1,17},{2,18},{3,19},{4,20},{5,21},{6,22},{7,23},{8,24},{9,... | collective-permute-start | bytes 36872 | tf_op jit(solution)/shard_map/ppermute | solution.py:20
  191.8 5.6 %collective-permute-start.12 = (f32[3,1,8,128]{3,2,1,0:T(8,128)S(1)}, f32[3,1,8,128]{3,2,1,0:T(8,128)S(1)}, u32[]{:S(2)}, u32[]{:S(2)}) collective-permute-start(f32[3,1,8,128]{3,2,1,0:T(8,128)S(1)} %get-tuple-element.34), channel_id=1, source_target_pairs={{16,0},{17,1},{18,2},{19,3},{20,4},{21,5},{22,6},{23,7},{24,8},{25... | collective-permute-start | bytes 36872 | tf_op jit(solution)/shard_map/ppermute | solution.py:23
  197.4 3.5 %collective-permute-start.15 = (f32[3,10,1,128]{3,2,1,0:T(1,128)S(1)}, f32[3,10,1,128]{3,2,1,0:T(1,128)S(1)}, u32[]{:S(2)}, u32[]{:S(2)}) collective-permute-start(f32[3,10,1,128]{3,2,1,0:T(1,128)S(1)} %get-tuple-element.25), channel_id=1, source_target_pairs={{0,4},{4,8},{8,12},{1,5},{5,9},{9,13},{2,6},{6,10},{10,14},{3,7},{... | collective-permute-start | bytes 46088 | tf_op jit(solution)/shard_map/ppermute | solution.py:20
  199.5 5.6 %collective-permute-start.14 = (f32[3,10,1,128]{3,2,1,0:T(1,128)S(1)}, f32[3,10,1,128]{3,2,1,0:T(1,128)S(1)}, u32[]{:S(2)}, u32[]{:S(2)}) collective-permute-start(f32[3,10,1,128]{3,2,1,0:T(1,128)S(1)} %get-tuple-element.26), channel_id=1, source_target_pairs={{4,0},{8,4},{12,8},{5,1},{9,5},{13,9},{6,2},{10,6},{14,10},{7,3},{... | collective-permute-start | bytes 46088 | tf_op jit(solution)/shard_map/ppermute | solution.py:23
  205.3 4.4 %collective-permute-start.16 = (f32[3,10,10,1]{3,2,1,0:T(8,128)S(1)}, f32[3,10,10,1]{3,2,1,0:T(8,128)S(1)}, u32[]{:S(2)}, u32[]{:S(2)}) collective-permute-start(f32[3,10,10,1]{3,2,1,0:T(8,128)S(1)} %get-tuple-element.19), channel_id=1, source_target_pairs={{1,0},{2,1},{3,2},{5,4},{6,5},{7,6},{9,8},{10,9},{11,10},{13,12},{... | collective-permute-start | bytes 3608 | tf_op jit(solution)/shard_map/ppermute | solution.py:23
  206.6 4.2 %collective-permute-start.17 = (f32[3,10,10,1]{3,2,1,0:T(8,128)S(1)}, f32[3,10,10,1]{3,2,1,0:T(8,128)S(1)}, u32[]{:S(2)}, u32[]{:S(2)}) collective-permute-start(f32[3,10,10,1]{3,2,1,0:T(8,128)S(1)} %get-tuple-element.20), channel_id=1, source_target_pairs={{0,1},{1,2},{2,3},{4,5},{5,6},{6,7},{8,9},{9,10},{10,11},{12,13},{... | collective-permute-start | bytes 3608 | tf_op jit(solution)/shard_map/ppermute | solution.py:20
where the time goes:
time: 261 us; the launch traced here: 260 us
  blocking collectives  137 us (52%)
  starting transfers between devices  40.7 us (16%)
  waiting for transfers between devices  28.8 us (11%)
  matrix products  21.5 us (8%)
  other arithmetic  12.9 us (5%)
  between operations  10.8 us (4%)
  local copies, waits for them, and re-layouts  8.15 us (3%)
    psum x3, blocking collectives, two_products(): lax.psum((jnp.sum(residual * residual), jnp.sum(residual * image)), ('gx'...  131 us
    ppermute x9, starting transfers between devices, with_halo(): lax.ppermute(lax.slice_in_dim(block, block.shape[dim] - width, None, axis...  29 us
    ppermute x9, waiting for transfers between devices, with_halo(): lax.ppermute(lax.slice_in_dim(block, 0, width, axis=dim), axis, backward)  25.2 us
    dot_general x2, matrix products, correction(): jnp.dot(polarization.reshape(row_count * 3, VOX), hartley, preferred_elem...  16.4 us
    ppermute x9, starting transfers between devices, with_halo(): lax.ppermute(lax.slice_in_dim(block, 0, width, axis=dim), axis, backward)  11.6 us
    reduce_sum x2, other arithmetic, correction(): jnp.sum(blocks * spectrum[:, None, :, :], axis=2).astype(jnp.bfloat16)  8.07 us
    all_gather x1, blocking collectives, per_device(): library = lax.all_gather(inverse_blocks, 'gx', axis=0, tiled=True)  6.23 us
  transfers between devices with their start and end apart: 18, of which 15 were waited for; matrix products, arithmetic and copies ran while one was open for 0% of the time, Pallas kernels for 0%

commit v1 on v0

--- a/solution.py
+++ b/solution.py
@@ -76,7 +76,9 @@
 
 
 def two_products(residual, image):
-    return lax.psum((jnp.sum(residual * residual), jnp.sum(residual * image)), ("gx", "gy", "gz"))
+    return lax.psum(
+        lax.psum((jnp.sum(residual * residual), jnp.sum(residual * image)), ("gy", "gz")), "gx"
+    )
 
 
 def per_device(source_field, cell_contrast, point_field, point_class, cell_kind, inverse_blocks):

time: 261 us -> 238 us (0.912)
  blocking collectives: 137 us -> 120 us
  starting transfers between devices: 40.7 us -> 34.5 us
    psum x3 -> x6, blocking collectives: 131 us -> 114 us  [the longest x3 97.6 us: two_products(): lax.psum((jnp.sum(residual * residual), jnp.sum(residual * image)), ('gy'...]
    ppermute x9, starting transfers between devices: 29 us -> 22.9 us  [with_halo(): lax.ppermute(lax.slice_in_dim(block, block.shape[dim] - width, None, axis...]
where the time goes in v1:
time: 238 us; the launch traced here: 237 us
  blocking collectives  120 us (50%)
  starting transfers between devices  34.5 us (14%)
  waiting for transfers between devices  28.8 us (12%)
  matrix products  21.5 us (9%)
  other arithmetic  12.9 us (5%)
  between operations  10.9 us (5%)
  local copies, waits for them, and re-layouts  8.16 us (3%)
    psum x3, blocking collectives, two_products(): lax.psum((jnp.sum(residual * residual), jnp.sum(residual * image)), ('gy'...  97.6 us
    ppermute x9, waiting for transfers between devices, with_halo(): lax.ppermute(lax.slice_in_dim(block, 0, width, axis=dim), axis, backward)  25.2 us
    ppermute x9, starting transfers between devices, with_halo(): lax.ppermute(lax.slice_in_dim(block, block.shape[dim] - width, None, axis...  22.9 us
    psum x3, blocking collectives, two_products(): lax.psum(lax.psum((jnp.sum(residual * residual), jnp.sum(residual * image...  16.7 us
    dot_general x2, matrix products, correction(): jnp.dot(polarization.reshape(row_count * 3, VOX), hartley, preferred_elem...  16.3 us
    ppermute x9, starting transfers between devices, with_halo(): lax.ppermute(lax.slice_in_dim(block, 0, width, axis=dim), axis, backward)  11.6 us
    reduce_sum x2, other arithmetic, correction(): jnp.sum(blocks * spectrum[:, None, :, :], axis=2).astype(jnp.bfloat16)  8.06 us
    all_gather x1, blocking collectives, per_device(): library = lax.all_gather(inverse_blocks, 'gx', axis=0, tiled=True)  6.23 us
  transfers between devices with their start and end apart: 18, of which 15 were waited for; matrix products, arithmetic and copies ran while one was open for 0% of the time, Pallas kernels for 0%

profile of v1, /device:TPU:0, one launch (start us, length us, event | category | flops | bytes accessed | tf_op | source)
XLA Modules:
  0.0 237.3 jit_solution(3420601430040013988)
XLA Ops:
  0.7 0.7 convert_bitcast_fusion
  1.3 0.7 compare_select_fusion
  2.0 6.2 %all_gather.3 = f32[2,4,3,3,512]{4,1,3,2,0:T(4,128)S(1)} all-gather(f32[1,4,3,3,512]{4,1,3,2,0:T(4,128)} %param.11), channel_id=1, replica_groups=mesh['gx'=2,'gy'=4,'gz'=4] {'gx'}, dimensions={0}, use_global_device_ids=true | all-gather | bytes 221184 | tf_op jit(solution)/shard_map/all_gather | solution.py:87
  8.2 0.1 copy.45
  8.3 1.2 copy.34
  9.6 0.2 copy.35
  9.8 4.7 %fusion.12 = f32[128,3,512]{2,0,1:T(8,128)S(1)} fusion(s32[512]{0:T(512)S(1)} %get-tuple-element.45, s32[512]{0:T(512)S(1)} %get-tuple-element.46, s32[512]{0:T(512)S(1)} %add_select_fusion.4, f32[128,3,512]{2,0,1:T(8,128)S(1)} %copy.35, f32[128,3]{0,1:T(4,128)S(1)} %convert_bitcast_fusion), kind=kOutput, calls=%fused_computation.24 | convolution fusion | flops 207224832 | bytes 1580544 | tf_op jit(solution)/shard_map/dot_general | solution.py:48
  14.5 1.5 copy.39
  16.0 2.4 %gather_fusion = f32[128,3,3,512]{3,2,1,0:T(4,128)S(1)} fusion(f32[8,3,3,512]{3,2,1,0:T(4,128)S(1)} %bitcast.21, s32[1024]{0:T(1024)S(1)} %pad_clamp_fusion), kind=kCustom, calls=%fused_computation | custom fusion | bytes 4719104 | tf_op jit(solution)/shard_map/gather | solution.py:67
  18.5 4.6 %multiply_reduce_fusion.1 = bf16[128,3,512]{2,1,0:T(4,128)(2,1)} fusion(f32[128,3,3,512]{3,2,1,0:T(4,128)S(1)} %gather_fusion, f32[128,3,512]{2,1,0:T(4,128)} %copy.39), kind=kLoop, calls=%fused_computation.2 | loop fusion | flops 983040 | bytes 3538944 | tf_op jit(solution)/shard_map/reduce_sum | solution.py:51
  23.1 11.6 %fusion.7 = f32[128,3,512]{2,0,1:T(8,128)} fusion(f32[128,3,512]{2,0,1:T(8,128)} %copy-done.1, s32[512]{0:T(512)S(1)} %get-tuple-element.45, s32[512]{0:T(512)S(1)} %get-tuple-element.46, s32[512]{0:T(512)S(1)} %add_select_fusion.4, bf16[128,3,512]{2,1,0:T(4,128)(2,1)} %multiply_reduce_fusion.1, f32[128,3]{0,1:T(4,128)S(1)} %convert_bitcast_fusion), kind=kOutput, calls=%fused_computation.21 | convolution fusion | flops 415039488 | bytes 1973760 | tf_op jit(solution)/shard_map/dot_general | solution.py:48
  34.7 1.7 copy.42
  36.4 3.5 %multiply_reduce_fusion = bf16[128,3,512]{2,1,0:T(4,128)(2,1)S(1)} fusion(f32[128,3,3,512]{3,2,1,0:T(4,128)S(1)} %gather_fusion, f32[128,3,512]{2,1,0:T(4,128)S(1)} %copy.42), kind=kLoop, calls=%fused_computation.1 | loop fusion | flops 983040 | bytes 3538944 | tf_op jit(solution)/shard_map/reduce_sum | solution.py:51
  39.9 5.2 %fusion.6 = (f32[128]{0:T(128)S(1)}, f32[128,3]{0,1:T(4,128)S(1)}) fusion(f32[128,3,512]{2,0,1:T(8,128)S(1)} %copy-done.2, s32[512]{0:T(512)S(1)} %get-tuple-element.45, s32[512]{0:T(512)S(1)} %get-tuple-element.46, s32[512]{0:T(512)S(1)} %add_select_fusion.4, bf16[128,3,512]{2,1,0:T(4,128)(2,1)S(1)} %multiply_reduce_fusion, ...), kind=kOutput, calls=%fused_computation.17 | convolution fusion | flops 208207360 | bytes 1189376 | tf_op jit(solution)/shard_map/dot_general | solution.py:52
  45.1 0.1 broadcast_in_dim.13
  45.2 0.1 broadcast_in_dim.14
  45.3 0.1 broadcast_in_dim.15
  45.5 3.9 %collective-permute-start.1 = (f32[3,1,8,128]{3,2,1,0:T(8,128)S(1)}, f32[3,1,8,128]{3,2,1,0:T(8,128)S(1)}, u32[]{:S(2)}, u32[]{:S(2)}) collective-permute-start(f32[3,1,8,128]{3,2,1,0:T(8,128)S(1)} %get-tuple-element.43), channel_id=1, source_target_pairs={{0,16},{1,17},{2,18},{3,19},{4,20},{5,21},{6,22},{7,23},{8,24},{9,... | collective-permute-start | bytes 36872 | tf_op jit(solution)/shard_map/ppermute | solution.py:20
  49.3 1.3 collective-permute-start
  50.6 0.1 collective-permute-done.1
  50.7 4.2 %collective-permute-done = f32[3,1,8,128]{3,2,1,0:T(8,128)S(1)} collective-permute-done((f32[3,1,8,128]{3,2,1,0:T(8,128)S(1)}, f32[3,1,8,128]{3,2,1,0:T(8,128)S(1)}, u32[]{:S(2)}, u32[]{:S(2)}) %collective-permute-start) | collective-permute-done | bytes 12320 | tf_op jit(solution)/shard_map/ppermute | solution.py:23
  55.0 3.5 %collective-permute-start.3 = (f32[3,10,1,128]{3,2,1,0:T(1,128)S(1)}, f32[3,10,1,128]{3,2,1,0:T(1,128)S(1)}, u32[]{:S(2)}, u32[]{:S(2)}) collective-permute-start(f32[3,10,1,128]{3,2,1,0:T(1,128)S(1)} %get-tuple-element.35), channel_id=1, source_target_pairs={{0,4},{4,8},{8,12},{1,5},{5,9},{9,13},{2,6},{6,10},{10,14},{3,7},{... | collective-permute-start | bytes 46088 | tf_op jit(solution)/shard_map/ppermute | solution.py:20
  58.5 1.3 collective-permute-start.2
  59.8 0.1 collective-permute-done.3
  59.9 4.2 %collective-permute-done.2 = f32[3,10,1,128]{3,2,1,0:T(1,128)S(1)} collective-permute-done((f32[3,10,1,128]{3,2,1,0:T(1,128)S(1)}, f32[3,10,1,128]{3,2,1,0:T(1,128)S(1)}, u32[]{:S(2)}, u32[]{:S(2)}) %collective-permute-start.2) | collective-permute-done | bytes 15392 | tf_op jit(solution)/shard_map/ppermute | solution.py:23
  64.1 0.1 fusion.70
  64.3 1.3 collective-permute-start.4
  65.6 3.0 %collective-permute-start.5 = (f32[3,10,10,1]{3,2,1,0:T(8,128)S(1)}, f32[3,10,10,1]{3,2,1,0:T(8,128)S(1)}, u32[]{:S(2)}, u32[]{:S(2)}) collective-permute-start(f32[3,10,10,1]{3,2,1,0:T(8,128)S(1)} %get-tuple-element.30), channel_id=1, source_target_pairs={{0,1},{1,2},{2,3},{4,5},{5,6},{6,7},{8,9},{9,10},{10,11},{12,13},{... | collective-permute-start | bytes 3608 | tf_op jit(solution)/shard_map/ppermute | solution.py:20
  68.8 0.1 add.235
  68.9 0.8 collective-permute-done.5
  69.7 0.8 multiply_reduce_fusion.7
  70.5 33.2 %all-reduce.2 = (f32[]{:T(128)}, f32[]{:T(128)}) all-reduce(f32[]{:T(128)} %get-tuple-element.9, f32[]{:T(128)} %get-tuple-element.8), channel_id=1, replica_groups=mesh['gx'=2,'gy'=4,'gz'=4] {'gy','gz'}, use_global_device_ids=true, to_apply=%region_4.5 | all-reduce | flops 2 | bytes 16 | tf_op jit(solution)/shard_map/psum | solution.py:80
  103.8 5.5 %all-reduce.5 = (f32[]{:T(128)}, f32[]{:T(128)}) all-reduce(f32[]{:T(128)} %get-tuple-element.14, f32[]{:T(128)} %get-tuple-element.15), channel_id=1, replica_groups=mesh['gx'=2,'gy'=4,'gz'=4] {'gx'}, use_global_device_ids=true, to_apply=%region_5.6 | all-reduce | flops 2 | bytes 16 | tf_op jit(solution)/shard_map/psum | solution.py:79
  110.7 1.9 collective-permute-start.7
  112.6 1.3 collective-permute-start.6
  113.9 0.1 collective-permute-done.7
  114.0 4.2 %collective-permute-done.6 = f32[3,1,8,128]{3,2,1,0:T(8,128)S(1)} collective-permute-done((f32[3,1,8,128]{3,2,1,0:T(8,128)S(1)}, f32[3,1,8,128]{3,2,1,0:T(8,128)S(1)}, u32[]{:S(2)}, u32[]{:S(2)}) %collective-permute-start.6) | collective-permute-done | bytes 12320 | tf_op jit(solution)/shard_map/ppermute | solution.py:23
  118.2 1.3 collective-permute-start.9
  119.5 1.3 collective-permute-start.8
  120.8 0.1 collective-permute-done.9
  120.9 4.2 %collective-permute-done.8 = f32[3,10,1,128]{3,2,1,0:T(1,128)S(1)} collective-permute-done((f32[3,10,1,128]{3,2,1,0:T(1,128)S(1)}, f32[3,10,1,128]{3,2,1,0:T(1,128)S(1)}, u32[]{:S(2)}, u32[]{:S(2)}) %collective-permute-start.8) | collective-permute-done | bytes 15392 | tf_op jit(solution)/shard_map/ppermute | solution.py:23
  125.2 0.1 fusion.69
  125.3 1.3 collective-permute-start.10
  126.6 3.0 %collective-permute-start.11 = (f32[3,10,10,1]{3,2,1,0:T(8,128)S(1)}, f32[3,10,10,1]{3,2,1,0:T(8,128)S(1)}, u32[]{:S(2)}, u32[]{:S(2)}) collective-permute-start(f32[3,10,10,1]{3,2,1,0:T(8,128)S(1)} %get-tuple-element.28), channel_id=1, source_target_pairs={{0,1},{1,2},{2,3},{4,5},{5,6},{6,7},{8,9},{9,10},{10,11},{12,13},{... | collective-permute-start | bytes 3608 | tf_op jit(solution)/shard_map/ppermute | solution.py:20
  129.7 1.1 collective-permute-done.11
  130.8 0.9 multiply_reduce_fusion.5
  131.6 32.2 %all-reduce.1 = (f32[]{:T(128)}, f32[]{:T(128)}) all-reduce(f32[]{:T(128)} %get-tuple-element.7, f32[]{:T(128)} %get-tuple-element.6), channel_id=1, replica_groups=mesh['gx'=2,'gy'=4,'gz'=4] {'gy','gz'}, use_global_device_ids=true, to_apply=%region_11.12 | all-reduce | flops 2 | bytes 16 | tf_op jit(solution)/shard_map/psum | solution.py:80
  163.8 5.6 %all-reduce.4 = (f32[]{:T(128)}, f32[]{:T(128)}) all-reduce(f32[]{:T(128)} %get-tuple-element.12, f32[]{:T(128)} %get-tuple-element.13), channel_id=1, replica_groups=mesh['gx'=2,'gy'=4,'gz'=4] {'gx'}, use_global_device_ids=true, to_apply=%region_12.13 | all-reduce | flops 2 | bytes 16 | tf_op jit(solution)/shard_map/psum | solution.py:79
  174.1 1.9 collective-permute-start.13
  176.0 1.3 collective-permute-start.12
  177.3 0.1 collective-permute-done.13
  177.3 4.2 %collective-permute-done.12 = f32[3,1,8,128]{3,2,1,0:T(8,128)S(1)} collective-permute-done((f32[3,1,8,128]{3,2,1,0:T(8,128)S(1)}, f32[3,1,8,128]{3,2,1,0:T(8,128)S(1)}, u32[]{:S(2)}, u32[]{:S(2)}) %collective-permute-start.12) | collective-permute-done | bytes 12320 | tf_op jit(solution)/shard_map/ppermute | solution.py:23
  181.6 1.3 collective-permute-start.15
  182.9 1.3 collective-permute-start.14
  184.2 0.1 collective-permute-done.15
  184.3 4.2 %collective-permute-done.14 = f32[3,10,1,128]{3,2,1,0:T(1,128)S(1)} collective-permute-done((f32[3,10,1,128]{3,2,1,0:T(1,128)S(1)}, f32[3,10,1,128]{3,2,1,0:T(1,128)S(1)}, u32[]{:S(2)}, u32[]{:S(2)}) %collective-permute-start.14) | collective-permute-done | bytes 15392 | tf_op jit(solution)/shard_map/ppermute | solution.py:23
  188.5 0.1 fusion.68
  188.7 1.3 collective-permute-start.16
  190.0 3.0 %collective-permute-start.17 = (f32[3,10,10,1]{3,2,1,0:T(8,128)S(1)}, f32[3,10,10,1]{3,2,1,0:T(8,128)S(1)}, u32[]{:S(2)}, u32[]{:S(2)}) collective-permute-start(f32[3,10,10,1]{3,2,1,0:T(8,128)S(1)} %get-tuple-element.26), channel_id=1, source_target_pairs={{0,1},{1,2},{2,3},{4,5},{5,6},{6,7},{8,9},{9,10},{10,11},{12,13},{... | collective-permute-start | bytes 3608 | tf_op jit(solution)/shard_map/ppermute | solution.py:20
  193.0 1.1 collective-permute-done.17
  194.1 0.8 multiply_reduce_fusion.3
  194.9 32.1 %all-reduce = (f32[]{:T(128)}, f32[]{:T(128)}) all-reduce(f32[]{:T(128)} %get-tuple-element.5, f32[]{:T(128)} %get-tuple-element.4), channel_id=1, replica_groups=mesh['gx'=2,'gy'=4,'gz'=4] {'gy','gz'}, use_global_device_ids=true, to_apply=%region_17.18 | all-reduce | flops 2 | bytes 16 | tf_op jit(solution)/shard_map/psum | solution.py:80
  227.1 5.5 %all-reduce.3 = (f32[]{:T(128)}, f32[]{:T(128)}) all-reduce(f32[]{:T(128)} %get-tuple-element.10, f32[]{:T(128)} %get-tuple-element.11), channel_id=1, replica_groups=mesh['gx'=2,'gy'=4,'gz'=4] {'gx'}, use_global_device_ids=true, to_apply=%region_18.19 | all-reduce | flops 2 | bytes 16 | tf_op jit(solution)/shard_map/psum | solution.py:79
  236.6 0.7 multiply_subtract_fusion
  (28 shorter events, 0.5 us)
Async XLA Ops:
  9.7 4.8 %copy-start.1 = (f32[128,3,512]{2,0,1:T(8,128)}, f32[128,3,512]{2,0,1:T(8,128)S(1)}, u32[]{:S(2)}) copy-start(f32[128,3,512]{2,0,1:T(8,128)S(1)} %copy.35) | copy-start | bytes 2359300
  34.7 5.2 %copy-start.2 = (f32[128,3,512]{2,0,1:T(8,128)S(1)}, f32[128,3,512]{2,0,1:T(8,128)}, u32[]{:S(2)}) copy-start(f32[128,3,512]{2,0,1:T(8,128)} %copy-done.1) | copy-start | bytes 2359300
  39.9 5.5 %copy-start = (f32[3,8,8,128]{3,2,1,0:T(8,128)S(1)}, f32[3,8,8,128]{3,2,1,0:T(8,128)}, u32[]{:S(2)}) copy-start(f32[3,8,8,128]{3,2,1,0:T(8,128)} %param.6) | copy-start | bytes 294916
  45.5 5.3 %collective-permute-start.1 = (f32[3,1,8,128]{3,2,1,0:T(8,128)S(1)}, f32[3,1,8,128]{3,2,1,0:T(8,128)S(1)}, u32[]{:S(2)}, u32[]{:S(2)}) collective-permute-start(f32[3,1,8,128]{3,2,1,0:T(8,128)S(1)} %get-tuple-element.43), channel_id=1, source_target_pairs={{0,16},{1,17},{2,18},{3,19},{4,20},{5,21},{6,22},{7,23},{8,24},{9,... | collective-permute-start | bytes 36872 | tf_op jit(solution)/shard_map/ppermute | solution.py:20
  49.3 5.6 %collective-permute-start = (f32[3,1,8,128]{3,2,1,0:T(8,128)S(1)}, f32[3,1,8,128]{3,2,1,0:T(8,128)S(1)}, u32[]{:S(2)}, u32[]{:S(2)}) collective-permute-start(f32[3,1,8,128]{3,2,1,0:T(8,128)S(1)} %get-tuple-element.44), channel_id=1, source_target_pairs={{16,0},{17,1},{18,2},{19,3},{20,4},{21,5},{22,6},{23,7},{24,8},{25... | collective-permute-start | bytes 36872 | tf_op jit(solution)/shard_map/ppermute | solution.py:23
  55.0 4.9 %collective-permute-start.3 = (f32[3,10,1,128]{3,2,1,0:T(1,128)S(1)}, f32[3,10,1,128]{3,2,1,0:T(1,128)S(1)}, u32[]{:S(2)}, u32[]{:S(2)}) collective-permute-start(f32[3,10,1,128]{3,2,1,0:T(1,128)S(1)} %get-tuple-element.35), channel_id=1, source_target_pairs={{0,4},{4,8},{8,12},{1,5},{5,9},{9,13},{2,6},{6,10},{10,14},{3,7},{... | collective-permute-start | bytes 46088 | tf_op jit(solution)/shard_map/ppermute | solution.py:20
  58.5 5.6 %collective-permute-start.2 = (f32[3,10,1,128]{3,2,1,0:T(1,128)S(1)}, f32[3,10,1,128]{3,2,1,0:T(1,128)S(1)}, u32[]{:S(2)}, u32[]{:S(2)}) collective-permute-start(f32[3,10,1,128]{3,2,1,0:T(1,128)S(1)} %get-tuple-element.36), channel_id=1, source_target_pairs={{4,0},{8,4},{12,8},{5,1},{9,5},{13,9},{6,2},{10,6},{14,10},{7,3},{... | collective-permute-start | bytes 46088 | tf_op jit(solution)/shard_map/ppermute | solution.py:23
  64.3 4.6 %collective-permute-start.4 = (f32[3,10,10,1]{3,2,1,0:T(8,128)S(1)}, f32[3,10,10,1]{3,2,1,0:T(8,128)S(1)}, u32[]{:S(2)}, u32[]{:S(2)}) collective-permute-start(f32[3,10,10,1]{3,2,1,0:T(8,128)S(1)} %get-tuple-element.29), channel_id=1, source_target_pairs={{1,0},{2,1},{3,2},{5,4},{6,5},{7,6},{9,8},{10,9},{11,10},{13,12},{... | collective-permute-start | bytes 3608 | tf_op jit(solution)/shard_map/ppermute | solution.py:23
  65.6 4.2 %collective-permute-start.5 = (f32[3,10,10,1]{3,2,1,0:T(8,128)S(1)}, f32[3,10,10,1]{3,2,1,0:T(8,128)S(1)}, u32[]{:S(2)}, u32[]{:S(2)}) collective-permute-start(f32[3,10,10,1]{3,2,1,0:T(8,128)S(1)} %get-tuple-element.30), channel_id=1, source_target_pairs={{0,1},{1,2},{2,3},{4,5},{5,6},{6,7},{8,9},{9,10},{10,11},{12,13},{... | collective-permute-start | bytes 3608 | tf_op jit(solution)/shard_map/ppermute | solution.py:20
  110.7 3.3 %collective-permute-start.7 = (f32[3,1,8,128]{3,2,1,0:T(8,128)S(1)}, f32[3,1,8,128]{3,2,1,0:T(8,128)S(1)}, u32[]{:S(2)}, u32[]{:S(2)}) collective-permute-start(f32[3,1,8,128]{3,2,1,0:T(8,128)S(1)} %get-tuple-element.41), channel_id=1, source_target_pairs={{0,16},{1,17},{2,18},{3,19},{4,20},{5,21},{6,22},{7,23},{8,24},{9,... | collective-permute-start | bytes 36872 | tf_op jit(solution)/shard_map/ppermute | solution.py:20
  112.6 5.6 %collective-permute-start.6 = (f32[3,1,8,128]{3,2,1,0:T(8,128)S(1)}, f32[3,1,8,128]{3,2,1,0:T(8,128)S(1)}, u32[]{:S(2)}, u32[]{:S(2)}) collective-permute-start(f32[3,1,8,128]{3,2,1,0:T(8,128)S(1)} %get-tuple-element.42), channel_id=1, source_target_pairs={{16,0},{17,1},{18,2},{19,3},{20,4},{21,5},{22,6},{23,7},{24,8},{25... | collective-permute-start | bytes 36872 | tf_op jit(solution)/shard_map/ppermute | solution.py:23
  118.2 2.7 %collective-permute-start.9 = (f32[3,10,1,128]{3,2,1,0:T(1,128)S(1)}, f32[3,10,1,128]{3,2,1,0:T(1,128)S(1)}, u32[]{:S(2)}, u32[]{:S(2)}) collective-permute-start(f32[3,10,1,128]{3,2,1,0:T(1,128)S(1)} %get-tuple-element.33), channel_id=1, source_target_pairs={{0,4},{4,8},{8,12},{1,5},{5,9},{9,13},{2,6},{6,10},{10,14},{3,7},{... | collective-permute-start | bytes 46088 | tf_op jit(solution)/shard_map/ppermute | solution.py:20
  119.5 5.6 %collective-permute-start.8 = (f32[3,10,1,128]{3,2,1,0:T(1,128)S(1)}, f32[3,10,1,128]{3,2,1,0:T(1,128)S(1)}, u32[]{:S(2)}, u32[]{:S(2)}) collective-permute-start(f32[3,10,1,128]{3,2,1,0:T(1,128)S(1)} %get-tuple-element.34), channel_id=1, source_target_pairs={{4,0},{8,4},{12,8},{5,1},{9,5},{13,9},{6,2},{10,6},{14,10},{7,3},{... | collective-permute-start | bytes 46088 | tf_op jit(solution)/shard_map/ppermute | solution.py:23
  125.3 4.4 %collective-permute-start.10 = (f32[3,10,10,1]{3,2,1,0:T(8,128)S(1)}, f32[3,10,10,1]{3,2,1,0:T(8,128)S(1)}, u32[]{:S(2)}, u32[]{:S(2)}) collective-permute-start(f32[3,10,10,1]{3,2,1,0:T(8,128)S(1)} %get-tuple-element.27), channel_id=1, source_target_pairs={{1,0},{2,1},{3,2},{5,4},{6,5},{7,6},{9,8},{10,9},{11,10},{13,12},{... | collective-permute-start | bytes 3608 | tf_op jit(solution)/shard_map/ppermute | solution.py:23
  126.6 4.2 %collective-permute-start.11 = (f32[3,10,10,1]{3,2,1,0:T(8,128)S(1)}, f32[3,10,10,1]{3,2,1,0:T(8,128)S(1)}, u32[]{:S(2)}, u32[]{:S(2)}) collective-permute-start(f32[3,10,10,1]{3,2,1,0:T(8,128)S(1)} %get-tuple-element.28), channel_id=1, source_target_pairs={{0,1},{1,2},{2,3},{4,5},{5,6},{6,7},{8,9},{9,10},{10,11},{12,13},{... | collective-permute-start | bytes 3608 | tf_op jit(solution)/shard_map/ppermute | solution.py:20
  174.1 3.3 %collective-permute-start.13 = (f32[3,1,8,128]{3,2,1,0:T(8,128)S(1)}, f32[3,1,8,128]{3,2,1,0:T(8,128)S(1)}, u32[]{:S(2)}, u32[]{:S(2)}) collective-permute-start(f32[3,1,8,128]{3,2,1,0:T(8,128)S(1)} %get-tuple-element.39), channel_id=1, source_target_pairs={{0,16},{1,17},{2,18},{3,19},{4,20},{5,21},{6,22},{7,23},{8,24},{9,... | collective-permute-start | bytes 36872 | tf_op jit(solution)/shard_map/ppermute | solution.py:20
  176.0 5.6 %collective-permute-start.12 = (f32[3,1,8,128]{3,2,1,0:T(8,128)S(1)}, f32[3,1,8,128]{3,2,1,0:T(8,128)S(1)}, u32[]{:S(2)}, u32[]{:S(2)}) collective-permute-start(f32[3,1,8,128]{3,2,1,0:T(8,128)S(1)} %get-tuple-element.40), channel_id=1, source_target_pairs={{16,0},{17,1},{18,2},{19,3},{20,4},{21,5},{22,6},{23,7},{24,8},{25... | collective-permute-start | bytes 36872 | tf_op jit(solution)/shard_map/ppermute | solution.py:23
  181.6 2.7 %collective-permute-start.15 = (f32[3,10,1,128]{3,2,1,0:T(1,128)S(1)}, f32[3,10,1,128]{3,2,1,0:T(1,128)S(1)}, u32[]{:S(2)}, u32[]{:S(2)}) collective-permute-start(f32[3,10,1,128]{3,2,1,0:T(1,128)S(1)} %get-tuple-element.31), channel_id=1, source_target_pairs={{0,4},{4,8},{8,12},{1,5},{5,9},{9,13},{2,6},{6,10},{10,14},{3,7},{... | collective-permute-start | bytes 46088 | tf_op jit(solution)/shard_map/ppermute | solution.py:20
  182.9 5.6 %collective-permute-start.14 = (f32[3,10,1,128]{3,2,1,0:T(1,128)S(1)}, f32[3,10,1,128]{3,2,1,0:T(1,128)S(1)}, u32[]{:S(2)}, u32[]{:S(2)}) collective-permute-start(f32[3,10,1,128]{3,2,1,0:T(1,128)S(1)} %get-tuple-element.32), channel_id=1, source_target_pairs={{4,0},{8,4},{12,8},{5,1},{9,5},{13,9},{6,2},{10,6},{14,10},{7,3},{... | collective-permute-start | bytes 46088 | tf_op jit(solution)/shard_map/ppermute | solution.py:23
  188.7 4.4 %collective-permute-start.16 = (f32[3,10,10,1]{3,2,1,0:T(8,128)S(1)}, f32[3,10,10,1]{3,2,1,0:T(8,128)S(1)}, u32[]{:S(2)}, u32[]{:S(2)}) collective-permute-start(f32[3,10,10,1]{3,2,1,0:T(8,128)S(1)} %get-tuple-element.25), channel_id=1, source_target_pairs={{1,0},{2,1},{3,2},{5,4},{6,5},{7,6},{9,8},{10,9},{11,10},{13,12},{... | collective-permute-start | bytes 3608 | tf_op jit(solution)/shard_map/ppermute | solution.py:23
  190.0 4.2 %collective-permute-start.17 = (f32[3,10,10,1]{3,2,1,0:T(8,128)S(1)}, f32[3,10,10,1]{3,2,1,0:T(8,128)S(1)}, u32[]{:S(2)}, u32[]{:S(2)}) collective-permute-start(f32[3,10,10,1]{3,2,1,0:T(8,128)S(1)} %get-tuple-element.26), channel_id=1, source_target_pairs={{0,1},{1,2},{2,3},{4,5},{5,6},{6,7},{8,9},{9,10},{10,11},{12,13},{... | collective-permute-start | bytes 3608 | tf_op jit(solution)/shard_map/ppermute | solution.py:20
